TPU v7x, 512 devices: a whole 4x8x8 slice. The times are simulated.
512 devices in a mesh: seq: 64 (over y, z), trk: 8 (over x, core).
Axes of the slice: x: 4, y: 8, z: 8, core: 2. Of those that a mesh axis runs over, the one named last changes fastest.
Arguments:
- embeddings: bfloat16 [4, 8192, 1920], P(None, 'seq', 'trk'), may hold values from -16 to 16
- head: bfloat16 [1920, 4096], P(None, 'trk'), may hold values from -0.125 to 0.125
- exon_starts: int32 [4, 128, 8], replicated, may hold values from 0 to 8184, as said below
- exon_lengths: int32 [4, 128, 8], replicated, may hold values from 1 to 8, as said below
- gene_owner: int32 [4, 128], replicated, may hold values from 0 to 63, as said below
- gene_targets: float32 [4, 256, 4096], P(None, 'seq', 'trk'), may hold values from 2 to 400, as said below
Outputs:
- gene_pred: float32 [4, 256, 4096], P(None, 'seq', 'trk')
- loss: float32 [4, 4096], P(None, 'trk')
- grad_head: float32 [1920, 4096], P('seq', 'trk')
Inputs may be any that keep to these rules, and one draw needn't show every extreme that they name: `exon_starts`: each gene has 8 exon blocks; blocks may intersect. Some block of each window starts at 0 and some at 8184. `exon_lengths`: some block of each window has length 8. `gene_owner`: in each window no owner holds more than 4 genes, and some owner holds exactly 4. `gene_targets`: entries of empty slots are read by nothing.
All inputs are finite; a program needn't handle non-finite values.
Results may differ from a plain program's by a relative error of at most 0.0041.
Values may be sent and summed in bfloat16 or wider, within the bound.
No kernel may reach another device: no remote copies, remote signals or barrier semaphores. Data moves between devices by JAX's collectives and lax.ppermute only.
A program may use at most 64 MiB of HBM per device.

v0:
```python
import jax
import jax.numpy as jnp
from jax import lax
from jax.sharding import PartitionSpec as P


def slot_table(gene_owner, capacity):
    genes = gene_owner.shape[1]
    same = gene_owner[:, :, None] == gene_owner[:, None, :]
    earlier = jnp.arange(genes)[None, :] < jnp.arange(genes)[:, None]
    ahead = jnp.sum((same & earlier[None]).astype(jnp.int32), axis=2)
    return gene_owner * capacity + ahead


def coverage(starts, lengths, positions):
    where_bin = positions[None, None, None, :]
    inside = (where_bin >= starts[..., None]) & (where_bin < (starts + lengths)[..., None])
    return jnp.sum(inside.astype(jnp.float32), axis=2)


def fold_sources(received):
    return jnp.sum(received, axis=1)


def per_device(embeddings, head, exon_starts, exon_lengths, gene_owner, gene_targets):
    seq_devices = lax.axis_size("seq")
    seq_place = lax.axis_index("seq")
    windows, bin_dev, _ = embeddings.shape
    genes = gene_owner.shape[1]
    capacity = gene_targets.shape[1]
    slot_total = seq_devices * capacity
    whole = lax.all_gather(embeddings, "trk", axis=2, tiled=True)
    logits = jnp.einsum("wbd,dt->wbt", whole, head, preferred_element_type=jnp.float32)
    pred = jax.nn.softplus(logits).astype(jnp.bfloat16)
    positions = seq_place * bin_dev + jnp.arange(bin_dev, dtype=jnp.int32)
    cover = coverage(exon_starts, exon_lengths, positions)
    slot_of = slot_table(gene_owner, capacity)
    onehot = (slot_of[..., None] == jnp.arange(slot_total, dtype=jnp.int32)).astype(jnp.float32)
    member = jnp.einsum("wgs,wgb->wsb", onehot, cover, precision=lax.Precision.HIGHEST).astype(
        jnp.bfloat16
    )
    valid = jnp.sum(onehot, axis=1)
    valid_here = lax.dynamic_slice_in_dim(valid, seq_place * capacity, capacity, 1)
    targets_here = gene_targets * valid_here[..., None]
    target_part = jnp.sum(targets_here, axis=1)
    partial_value = jnp.einsum("wsb,wbt->wst", member, pred, preferred_element_type=jnp.float32)
    blocks = partial_value.reshape(windows, seq_devices, capacity, partial_value.shape[2])
    gene_here = fold_sources(lax.all_to_all(blocks, "seq", split_axis=1, concat_axis=1, tiled=True))
    safe = jnp.where(valid_here[..., None] > 0, gene_here, 1.0)
    fit_part = jnp.sum(targets_here * jnp.log(safe), axis=1)
    total, target_sum, fit = lax.psum((jnp.sum(gene_here, axis=1), target_part, fit_part), "seq")
    scale_rows = (genes / target_sum)[:, None, :]
    gene_grad = (
        scale_rows
        * (
            valid_here[..., None] * (0.2 + 0.8 * target_sum / total)[:, None, :]
            - targets_here / safe
        )
    ).astype(jnp.bfloat16)
    bin_grad = jnp.einsum(
        "wsb,wst->wbt",
        member,
        lax.all_gather(gene_grad, "seq", axis=1, tiled=True),
        preferred_element_type=jnp.float32,
    )
    logit_grad = (bin_grad * jax.nn.sigmoid(logits)).astype(jnp.bfloat16)
    grad_head = lax.psum_scatter(
        jnp.einsum("wbd,wbt->dt", whole, logit_grad, preferred_element_type=jnp.float32),
        "seq",
        scatter_dimension=0,
        tiled=True,
    )
    log_total = jnp.log(total)
    loss = (-fit + target_sum * log_total + 0.2 * (total - target_sum * log_total)) / target_sum
    return (gene_here, loss, grad_head)


def solution(mesh):
    return jax.shard_map(
        per_device,
        mesh=mesh,
        in_specs=(P(None, "seq", "trk"), P(None, "trk"), P(), P(), P(), P(None, "seq", "trk")),
        out_specs=(P(None, "seq", "trk"), P(None, "trk"), P("seq", "trk")),
        check_vma=False,
    )
```

profile of v0, /device:TPU:2, one launch (start us, length us, event | category | flops | bytes accessed | tf_op | source)
XLA Modules:
  0.0 664.6 jit_solution(17121487797619391338)
XLA Ops:
  7.2 0.7 all-gather.3.cloned.1.call-update
  7.9 0.8 copy.28
  8.8 0.7 add.46
  9.7 1.0 convert_reduce_fusion.2
  10.7 0.7 multiply_add_fusion
  11.4 1.4 convert_reduce_fusion
  12.8 0.4 convolution_convert_fusion
  13.2 30.7 %all-gather.3.cloned.1.call-done = bf16[4,128,1920]{1,2,0:T(8,128)(2,1)} async-done(((bf16[4,128,240]{1,2,0:T(8,128)(2,1)}), bf16[4,128,1920]{1,2,0:T(8,128)(2,1)}) %all-gather.3.cloned.1.call-update) | async-done | bytes 1966096 | tf_op jit(solution)/shard_map/all_gather | solution.py:32
  43.9 2.8 fusion.13
  46.8 2.2 fusion.9
  48.9 2.9 reshape.35
  51.8 3.5 copy.30
  55.4 13.6 %all-to-all-start = ((f32[4,64,4,512]{3,2,0,1:T(4,128)}), f32[4,64,4,512]{3,2,0,1:T(4,128)}, u32[]{:S(2)}, u32[]{:S(2)}) async-start(f32[4,64,4,512]{3,2,0,1:T(4,128)} %copy.30), calls=%async_computation | async-start | bytes 4194304 | tf_op jit(solution)/shard_map/all_to_all | solution.py:48
  69.2 51.5 %all-to-all-done = f32[4,64,4,512]{3,2,0,1:T(4,128)} async-done(((f32[4,64,4,512]{3,2,0,1:T(4,128)}), f32[4,64,4,512]{3,2,0,1:T(4,128)}, u32[]{:S(2)}, u32[]{:S(2)}) %all-to-all-start) | async-done | bytes 2097184 | tf_op jit(solution)/shard_map/all_to_all | solution.py:48
  120.7 2.1 fusion.20
  122.9 282.3 %all-reduce.1 = (f32[4,512]{1,0:T(4,128)S(1)}, f32[4,512]{1,0:T(4,128)S(1)}, f32[4,512]{1,0:T(4,128)S(1)}) all-reduce(f32[4,512]{1,0:T(4,128)S(1)} %get-tuple-element.18, f32[4,512]{1,0:T(4,128)S(1)} %get-tuple-element.15, f32[4,512]{1,0:T(4,128)S(1)} %get-tuple-element.17), channel_id=1, replica_groups=mesh['seq'=64,'trk'=8] {'seq'}, use_global_device_ids=true, to_apply=%region_7.8 | all-reduce | flops 6144 | bytes 49152 | tf_op jit(solution)/shard_map/psum | solution.py:51
  405.2 0.6 fusion.16
  405.9 0.6 copy.31
  406.6 76.9 %all-gather.5.cloned.1.call-done = bf16[4,256,512]{2,0,1:T(4,128)(2,1)} async-done(((bf16[4,4,512]{2,0,1:T(4,128)(2,1)}), bf16[4,256,512]{2,0,1:T(4,128)(2,1)}) %all-gather.5.cloned.1.call-update) | async-done | bytes 1048592 | tf_op jit(solution)/shard_map/all_gather | solution.py:63
  483.5 5.5 convolution_bitcast_fusion
  489.0 1.3 dynamic-slice
  490.9 165.2 %all-reduce.4.cloned.1.call-done = f32[1920,512]{0,1:T(8,128)} async-done(((f32[1920,512]{0,1:T(8,128)}), f32[1920,512]{0,1:T(8,128)}) %all-reduce.4.cloned.1.call-update) | async-done | bytes 3932176
  656.1 1.2 constant_dynamic-slice_fusion
  657.3 0.8 copy.35
  (18 shorter events, 0.8 us)
Async XLA Ops:
  7.2 36.7 %copy-start = (bf16[1920,512]{1,0:T(8,128)(2,1)S(1)}, bf16[1920,512]{1,0:T(8,128)(2,1)}, u32[]{:S(2)}) copy-start(bf16[1920,512]{1,0:T(8,128)(2,1)} %param.7) | copy-start | bytes 5898244
  7.2 36.7 %all-gather.3.cloned.1.call-start = ((), (), s32[]{:S(2)}) async-start(), calls=%async_computation.1 | async-start | bytes 2211840 | tf_op jit(solution)/shard_map/all_gather | solution.py:32
  55.4 65.3 %all-to-all-start = ((f32[4,64,4,512]{3,2,0,1:T(4,128)}), f32[4,64,4,512]{3,2,0,1:T(4,128)}, u32[]{:S(2)}, u32[]{:S(2)}) async-start(f32[4,64,4,512]{3,2,0,1:T(4,128)} %copy.30), calls=%async_computation | async-start | bytes 4194304 | tf_op jit(solution)/shard_map/all_to_all | solution.py:48
  68.9 53.8 %copy-start.2 = (f32[4,4,512]{2,1,0:T(4,128)S(1)}, f32[4,4,512]{2,1,0:T(4,128)}, u32[]{:S(2)}) copy-start(f32[4,4,512]{2,1,0:T(4,128)} %param.11) | copy-start | bytes 98308
  68.9 414.6 %all-gather.5.cloned.1.call-start = ((), (), s32[]{:S(2)}) async-start(), calls=%async_computation.2 | async-start | bytes 1064960 | tf_op jit(solution)/shard_map/all_gather | solution.py:63
  122.7 366.2 %copy-start.1 = (f32[4,4,512]{2,1,0:T(4,128)}, f32[4,4,512]{2,1,0:T(4,128)S(1)}, u32[]{:S(2)}) copy-start(f32[4,4,512]{2,1,0:T(4,128)S(1)} %get-tuple-element.16) | copy-start | bytes 98308
  406.5 249.6 %all-reduce.4.cloned.1.call-start = ((), (), s32[]{:S(2)}) async-start(), calls=%async_computation.3 | async-start | bytes 7864320
Sparse Core Ops, SparseCore 0:
  10.1 33.7 all-gather.2
  406.7 76.7 all-gather.4
  489.1 166.9 all-reduce.3
where the time goes:
time: 665 us
  waiting for transfers between devices  325 us (49%)
  blocking collectives  282 us (42%)
  between operations  14.5 us (2%)
  starting transfers between devices  13.7 us (2%)
  local copies, waits for them, and re-layouts  11.2 us (2%)
  matrix products  10.9 us (2%)
  other arithmetic  7 us (1%)
    psum x1, blocking collectives, per_device(): lax.psum((jnp.sum(gene_here, axis=1), target_part, fit_part), 'seq')  282 us
    unnamed x4, waiting for transfers between devices  166 us
    all_gather x1, waiting for transfers between devices, per_device(): lax.all_gather(gene_grad, 'seq', axis=1, tiled=True)  76.9 us
    all_to_all x1, waiting for transfers between devices, per_device(): lax.all_to_all(blocks, 'seq', split_axis=1, concat_axis=1, tiled=True)  51.5 us
    all_gather x1, waiting for transfers between devices, per_device(): whole = lax.all_gather(embeddings, 'trk', axis=2, tiled=True)  30.7 us
    all_to_all x1, starting transfers between devices, per_device(): lax.all_to_all(blocks, 'seq', split_axis=1, concat_axis=1, tiled=True)  13.6 us
  transfers between devices with their start and end apart: 4, of which 4 were waited for; matrix products, arithmetic and copies ran while one was open for 1% of the time, Pallas kernels for 0%

commit v1 on v0

--- a/solution.py
+++ b/solution.py
@@ -57,11 +57,21 @@
             - targets_here / safe
         )
     ).astype(jnp.bfloat16)
+
+    def see_unit(page, array_dim):
+        mesh_ax = "seq"
+        full_n = lax.axis_size(mesh_ax)
+        w_next = lax.all_to_all(
+            jnp.tile(page, [full_n if dev_i == array_dim else 1 for dev_i in range(page.ndim)]),
+            mesh_ax,
+            tiled=True,
+            concat_axis=array_dim,
+            split_axis=array_dim,
+        )
+        return w_next
+
     bin_grad = jnp.einsum(
-        "wsb,wst->wbt",
-        member,
-        lax.all_gather(gene_grad, "seq", axis=1, tiled=True),
-        preferred_element_type=jnp.float32,
+        "wsb,wst->wbt", member, see_unit(gene_grad, 1), preferred_element_type=jnp.float32
     )
     logit_grad = (bin_grad * jax.nn.sigmoid(logits)).astype(jnp.bfloat16)
     grad_head = lax.psum_scatter(

time: 665 us -> 615 us (0.925)
  waiting for transfers between devices: 325 us -> 246 us
  blocking collectives: 282 us -> 311 us
    all_gather x1 -> x0, waiting for transfers between devices: 76.9 us -> none  [per_device(): lax.all_gather(gene_grad, 'seq', axis=1, tiled=True)]
    all_to_all x0 -> x1, blocking collectives: none -> 26.6 us  [see_unit(): lax.all_to_all(jnp.tile(page, [full_n if dev_i == array_dim else 1 for de...]
    unnamed x4 -> x3, waiting for transfers between devices: 166 us -> 164 us
  transfers between devices with their start and end apart: 4 -> 3, of which waited for: 4 -> 3; matrix products, arithmetic and copies ran while one was open for 1% -> 1% of each run, Pallas kernels for 0% -> 0%
where the time goes in v1:
time: 615 us
  blocking collectives  311 us (51%)
  waiting for transfers between devices  246 us (40%)
  between operations  14.8 us (2%)
  starting transfers between devices  13.6 us (2%)
  local copies, waits for them, and re-layouts  11.1 us (2%)
  matrix products  10.9 us (2%)
  other arithmetic  7 us (1%)
    psum x1, blocking collectives, per_device(): lax.psum((jnp.sum(gene_here, axis=1), target_part, fit_part), 'seq')  285 us
    unnamed x3, waiting for transfers between devices  164 us
    all_to_all x1, waiting for transfers between devices, per_device(): lax.all_to_all(blocks, 'seq', split_axis=1, concat_axis=1, tiled=True)  51.5 us
    all_gather x1, waiting for transfers between devices, per_device(): whole = lax.all_gather(embeddings, 'trk', axis=2, tiled=True)  30.7 us
    all_to_all x1, blocking collectives, see_unit(): lax.all_to_all(jnp.tile(page, [full_n if dev_i == array_dim else 1 for de...  26.6 us
    all_to_all x1, starting transfers between devices, per_device(): lax.all_to_all(blocks, 'seq', split_axis=1, concat_axis=1, tiled=True)  13.6 us
  transfers between devices with their start and end apart: 3, of which 3 were waited for; matrix products, arithmetic and copies ran while one was open for 1% of the time, Pallas kernels for 0%

profile of v1, /device:TPU:2, one launch (start us, length us, event | category | flops | bytes accessed | tf_op | source)
XLA Modules:
  0.0 614.8 jit_solution(17201438990222543362)
XLA Ops:
  7.2 0.7 all-gather.2.cloned.1.call-update
  7.9 0.8 copy.19
  8.8 0.7 add.46
  9.7 1.0 convert_reduce_fusion.2
  10.7 0.7 multiply_add_fusion
  11.4 1.4 convert_reduce_fusion
  12.8 0.4 convolution_convert_fusion
  13.2 30.7 %all-gather.2.cloned.1.call-done = bf16[4,128,1920]{1,2,0:T(8,128)(2,1)} async-done(((bf16[4,128,240]{1,2,0:T(8,128)(2,1)}), bf16[4,128,1920]{1,2,0:T(8,128)(2,1)}) %all-gather.2.cloned.1.call-update) | async-done | bytes 1966096 | tf_op jit(solution)/shard_map/all_gather | solution.py:32
  43.9 2.8 fusion.13
  46.8 2.2 fusion.9
  48.9 2.9 reshape.39
  51.8 3.5 copy.21
  55.4 13.6 %all-to-all-start = ((f32[4,64,4,512]{3,2,0,1:T(4,128)}), f32[4,64,4,512]{3,2,0,1:T(4,128)}, u32[]{:S(2)}, u32[]{:S(2)}) async-start(f32[4,64,4,512]{3,2,0,1:T(4,128)} %copy.21), calls=%async_computation | async-start | bytes 4194304 | tf_op jit(solution)/shard_map/all_to_all | solution.py:48
  69.2 51.5 %all-to-all-done = f32[4,64,4,512]{3,2,0,1:T(4,128)} async-done(((f32[4,64,4,512]{3,2,0,1:T(4,128)}), f32[4,64,4,512]{3,2,0,1:T(4,128)}, u32[]{:S(2)}, u32[]{:S(2)}) %all-to-all-start) | async-done | bytes 2097184 | tf_op jit(solution)/shard_map/all_to_all | solution.py:48
  120.7 2.1 fusion.20
  122.9 284.7 %all-reduce.1 = (f32[4,512]{1,0:T(4,128)S(1)}, f32[4,512]{1,0:T(4,128)S(1)}, f32[4,512]{1,0:T(4,128)S(1)}) all-reduce(f32[4,512]{1,0:T(4,128)S(1)} %get-tuple-element.15, f32[4,512]{1,0:T(4,128)S(1)} %get-tuple-element.12, f32[4,512]{1,0:T(4,128)S(1)} %get-tuple-element.14), channel_id=1, replica_groups=mesh['seq'=64,'trk'=8] {'seq'}, use_global_device_ids=true, to_apply=%region_7.8 | all-reduce | flops 6144 | bytes 49152 | tf_op jit(solution)/shard_map/psum | solution.py:51
  407.6 0.6 fusion.16
  408.3 0.5 tile.4
  408.8 26.6 %all_to_all.10 = bf16[4,256,512]{2,0,1:T(4,128)(2,1)} all-to-all(bf16[4,256,512]{2,0,1:T(4,128)(2,1)S(1)} %bitcast.18), channel_id=1, replica_groups=mesh['seq'=64,'trk'=8] {'seq'}, dimensions={1} | all-to-all | bytes 2097152 | tf_op jit(solution)/shard_map/all_to_all | solution.py:64
  435.5 5.5 convolution_bitcast_fusion
  441.0 1.3 dynamic-slice
  442.9 163.1 %all-reduce.4.cloned.1.call-done = f32[1920,512]{0,1:T(8,128)} async-done(((f32[1920,512]{0,1:T(8,128)}), f32[1920,512]{0,1:T(8,128)}) %all-reduce.4.cloned.1.call-update) | async-done | bytes 3932176
  606.0 1.2 constant_dynamic-slice_fusion
  607.2 0.8 copy.26
  (17 shorter events, 0.7 us)
Async XLA Ops:
  7.2 36.7 %copy-start = (bf16[1920,512]{1,0:T(8,128)(2,1)S(1)}, bf16[1920,512]{1,0:T(8,128)(2,1)}, u32[]{:S(2)}) copy-start(bf16[1920,512]{1,0:T(8,128)(2,1)} %param.7) | copy-start | bytes 5898244
  7.2 36.7 %all-gather.2.cloned.1.call-start = ((), (), s32[]{:S(2)}) async-start(), calls=%async_computation.2 | async-start | bytes 2211840 | tf_op jit(solution)/shard_map/all_gather | solution.py:32
  55.4 65.3 %all-to-all-start = ((f32[4,64,4,512]{3,2,0,1:T(4,128)}), f32[4,64,4,512]{3,2,0,1:T(4,128)}, u32[]{:S(2)}, u32[]{:S(2)}) async-start(f32[4,64,4,512]{3,2,0,1:T(4,128)} %copy.21), calls=%async_computation | async-start | bytes 4194304 | tf_op jit(solution)/shard_map/all_to_all | solution.py:48
  68.9 53.8 %copy-start.2 = (f32[4,4,512]{2,1,0:T(4,128)S(1)}, f32[4,4,512]{2,1,0:T(4,128)}, u32[]{:S(2)}) copy-start(f32[4,4,512]{2,1,0:T(4,128)} %param.11) | copy-start | bytes 98308
  68.9 537.1 %all-reduce.4.cloned.1.call-start = ((), (), s32[]{:S(2)}) async-start(), calls=%async_computation.3 | async-start | bytes 7864320
  122.7 318.2 %copy-start.1 = (f32[4,4,512]{2,1,0:T(4,128)}, f32[4,4,512]{2,1,0:T(4,128)S(1)}, u32[]{:S(2)}) copy-start(f32[4,4,512]{2,1,0:T(4,128)S(1)} %get-tuple-element.13) | copy-start | bytes 98308
Sparse Core Ops, SparseCore 0:
  10.1 33.7 all-gather.1
  441.1 164.8 all-reduce.3
